TPU v7x, 256 devices: a whole 4x4x8 slice. The times are simulated.
256 devices in a mesh: leaf: 32 (over y, z), panel: 8 (over x, core).
Axes of the slice: x: 4, y: 4, z: 8, core: 2. Of those that a mesh axis runs over, the one named last changes fastest.
Arguments:
- child_front: float32 [32, 2, 8, 128, 2048], P('leaf', None, 'panel'), as said below
- parent_entries: float32 [32, 4, 8, 128, 512], P('leaf', None, 'panel'), as said below
- parent_of: int32 [32], replicated, may hold values from 0 to 31
- owner_slot: int32 [32], replicated, may hold values from 0 to 31, each once
- front_blocks: int32 [32], replicated, may hold values from 8 to 32, as said below
- block_lists: int32 [32, 8], replicated, may hold values from 0 to 31, as said below
Outputs:
- child_factor: float32 [32, 2, 8, 128, 1024], P('leaf', None, 'panel')
- parent_factor: float32 [32, 4, 8, 128, 512], P('leaf', None, 'panel')
Inputs may be any that keep to these rules, and one draw needn't show every extreme that they name: `front_blocks`: each entry is a multiple of the panel axis size; the largest equals 32. `block_lists`: the entries of a row are distinct, each below front_blocks of the child's parent, and entry k leaves the same remainder as k when divided by the panel axis size. `child_front`: symmetric, with a positive definite leading block of every front. `parent_entries`: the leading 512 rows form a symmetric positive definite block.
All inputs are finite; a program needn't handle non-finite values.
Results may differ from a plain program's by a relative error of at most 0.00044.
Values may be sent and summed in bfloat16 or wider, within the bound.
No kernel may reach another device: no remote copies, remote signals or barrier semaphores. Data moves between devices by JAX's collectives and lax.ppermute only.
A program may use at most 128 MiB of HBM per device.

v0:
```python
import jax
import jax.numpy as jnp
from jax import lax
from jax.sharding import PartitionSpec as P

BLK = 128
PANEL = 512
WC = 2048
PC = 1024
CBB = 8


def place_columns(block_rows, block_map):
    count_in = block_rows.shape[0]
    row_slots = block_rows.shape[1]
    pivot_blocks = PANEL // BLK
    onehot = (block_map[:, :, None] == jnp.arange(pivot_blocks)[None, None, :]).astype(jnp.bfloat16)
    split_blocks = block_rows.reshape(count_in, row_slots, BLK, CBB, BLK)
    placed = jnp.einsum(
        "muvkc,mkb->muvbc", split_blocks, onehot, preferred_element_type=jnp.float32
    )
    return placed.reshape(count_in, row_slots, BLK, PANEL)


def place_rows(assembled, placed, block_map, destination, panel_count, panel_index, leaf_index):
    count_in = placed.shape[0]
    row_slots = placed.shape[1]
    parent_slots = assembled.shape[0]
    grouped = block_map.reshape(count_in, row_slots, panel_count)
    pick = (jnp.arange(panel_count) == panel_index).astype(jnp.int32)
    row_blocks = jnp.sum(grouped * pick[None, None, :], axis=2)
    target = row_blocks[:, :, None] // panel_count == jnp.arange(parent_slots)[None, None, :]
    target = jnp.logical_and(target, (destination == leaf_index)[:, None, None]).astype(jnp.float32)
    return assembled + jnp.einsum("muvx,mut->tvx", placed, target, precision=lax.Precision.HIGHEST)


def on_device(child_front, parent_entries, parent_of, owner_slot, front_blocks, block_lists):
    panel_count = lax.axis_size("panel")
    panel_index = lax.axis_index("panel")
    leaf_index = lax.axis_index("leaf")
    row_slots = child_front.shape[1]
    parent_slots = parent_entries.shape[1]
    local_rows = child_front.reshape(row_slots * BLK, WC)
    factors = []
    for first_col in range(0, PC, PANEL):
        trailing = first_col + PANEL
        column = local_rows[:, first_col:trailing]
        gathered = lax.all_gather(
            column.reshape(row_slots, 1, BLK, PANEL), "panel", axis=1, tiled=True
        )
        gathered = gathered.reshape(WC, PANEL)
        pivot_block = jnp.linalg.cholesky(gathered[first_col:trailing])
        all_rows = jax.scipy.linalg.solve_triangular(pivot_block, gathered.T, lower=True).T
        all_rows = jnp.where(jnp.arange(WC)[:, None] >= first_col, all_rows, 0.0)
        own_rows = lax.dynamic_slice_in_dim(
            all_rows.reshape(row_slots, panel_count, BLK, PANEL), panel_index, 1, 1
        )
        own_rows = own_rows.reshape(row_slots * BLK, PANEL)
        update = jnp.dot(own_rows, all_rows[trailing:].T, precision=lax.Precision.HIGHEST)
        local_rows = jnp.concatenate(
            [local_rows[:, :trailing], local_rows[:, trailing:] - update], axis=1
        )
        factors.append(own_rows)
    child_factor = jnp.concatenate(factors, axis=1).reshape(1, row_slots, 1, BLK, PC)
    first_cb = PC // (BLK * panel_count)
    contribution = local_rows.reshape(row_slots, BLK, WC)[first_cb:, :, PC:].astype(jnp.bfloat16)
    parent_hits = (parent_of[:, None] == jnp.arange(owner_slot.shape[0])[None, :]).astype(jnp.int32)
    slot_of_child = jnp.sum(parent_hits * owner_slot[None, :], axis=1)
    live_mine = jnp.sum(jnp.where(owner_slot == leaf_index, front_blocks, 0))
    entries = parent_entries.reshape(parent_slots, BLK, PANEL)
    global_block = jnp.arange(parent_slots) * panel_count + panel_index
    initial = jnp.where((global_block < live_mine)[:, None, None], entries, 0.0)
    placed = place_columns(
        lax.all_gather(contribution[None], "leaf", axis=0, tiled=True), block_lists
    )
    assembled = place_rows(
        initial, placed, block_lists, slot_of_child, panel_count, panel_index, leaf_index
    )
    stacked = lax.all_gather(assembled[0], "panel", axis=0, tiled=True)
    pivot_block = jnp.linalg.cholesky(stacked[:PANEL])
    parent_rows = assembled.reshape(parent_slots * BLK, PANEL)
    parent_factor = jax.scipy.linalg.solve_triangular(pivot_block, parent_rows.T, lower=True).T
    return (child_factor, parent_factor.reshape(1, parent_slots, 1, BLK, PANEL))


def solution(mesh):
    in_specs = (
        P("leaf", None, "panel", None, None),
        P("leaf", None, "panel", None, None),
        P(),
        P(),
        P(),
        P(),
    )
    out_specs = (P("leaf", None, "panel", None, None), P("leaf", None, "panel", None, None))
    return jax.shard_map(
        on_device, mesh=mesh, in_specs=in_specs, out_specs=out_specs, check_vma=False
    )
```

profile of v0, /device:TPU:1, one launch (start us, length us, event | category | flops | bytes accessed | tf_op | source)
XLA Modules:
  0.0 736.7 jit_solution(10436099563935229929)
XLA Ops:
  9.2 40.2 %all-gather.7.cloned.1.call-done = f32[2,8,128,512]{3,2,0,1:T(8,128)} async-done(((f32[2,1,128,512]{3,2,0,1:T(8,128)}), f32[2,8,128,512]{3,2,0,1:T(8,128)}) %all-gather.7.cloned.1.call-update) | async-done | bytes 4194320 | tf_op jit(solution)/shard_map/all_gather | solution.py:48
  62.7 11.7 %cholesky.374 = f32[128,128]{1,0:T(8,128)S(1)} custom-call(f32[128,128]{1,0:T(8,128)S(1)} %cholesky.586), custom_call_target="Cholesky" | custom-call | tf_op jit(solution)/shard_map/jit(cholesky)/cholesky | solution.py:52
  74.5 9.8 %custom-call.35 = f32[1,128,128]{1,2,0:T(8,128)S(1)} custom-call(f32[1,128,128]{2,1,0:T(8,128)S(1)} %get-tuple-element.103), custom_call_target="InvertDiagBlocksLowerTriangular" | custom-call | tf_op jit(solution)/shard_map/jit(cholesky)/cholesky | solution.py:52
  85.1 11.9 %cholesky.393 = f32[128,128]{1,0:T(8,128)S(1)} custom-call(f32[128,128]{1,0:T(8,128)S(1)} %cholesky.590), custom_call_target="Cholesky" | custom-call | tf_op jit(solution)/shard_map/jit(cholesky)/cholesky | solution.py:52
  97.0 9.8 %custom-call.36 = f32[1,128,128]{1,2,0:T(8,128)S(1)} custom-call(f32[1,128,128]{2,1,0:T(8,128)S(1)} %get-tuple-element.100), custom_call_target="InvertDiagBlocksLowerTriangular" | custom-call | tf_op jit(solution)/shard_map/jit(cholesky)/cholesky | solution.py:52
  107.5 11.7 %cholesky.414 = f32[128,128]{1,0:T(8,128)S(1)} custom-call(f32[128,128]{1,0:T(8,128)S(1)} %cholesky.595), custom_call_target="Cholesky" | custom-call | tf_op jit(solution)/shard_map/jit(cholesky)/cholesky | solution.py:52
  119.9 9.8 %custom-call.37 = f32[1,128,128]{1,2,0:T(8,128)S(1)} custom-call(f32[1,128,128]{2,1,0:T(8,128)S(1)} %get-tuple-element.97), custom_call_target="InvertDiagBlocksLowerTriangular" | custom-call | tf_op jit(solution)/shard_map/jit(cholesky)/cholesky | solution.py:52
  130.3 12.1 %cholesky.431 = f32[128,128]{1,0:T(8,128)S(1)} custom-call(f32[128,128]{1,0:T(8,128)S(1)} %convolution_subtract_fusion.15), custom_call_target="Cholesky" | custom-call | tf_op jit(solution)/shard_map/jit(cholesky)/cholesky | solution.py:52
  154.5 39.3 %custom-call.38 = f32[4,128,128]{1,2,0:T(8,128)S(1)} custom-call(f32[4,128,128]{2,1,0:T(8,128)S(1)} %get-tuple-element.26), custom_call_target="InvertDiagBlocksLowerTriangular" | custom-call | tf_op jit(solution)/shard_map/jit(_solve_triangular)/triangular_solve | solution.py:53
  213.6 33.6 %all-gather.9.cloned.1.call-done = f32[2,8,128,512]{3,2,0,1:T(8,128)} async-done(((f32[2,1,128,512]{3,2,0,1:T(8,128)}), f32[2,8,128,512]{3,2,0,1:T(8,128)}) %all-gather.9.cloned.1.call-update) | async-done | bytes 4194320 | tf_op jit(solution)/shard_map/all_gather | solution.py:48
  263.9 11.7 %cholesky.446 = f32[128,128]{1,0:T(8,128)S(1)} custom-call(f32[128,128]{1,0:T(8,128)S(1)} %cholesky.599), custom_call_target="Cholesky" | custom-call | tf_op jit(solution)/shard_map/jit(cholesky)/cholesky | solution.py:52
  275.7 9.8 %custom-call.39 = f32[1,128,128]{1,2,0:T(8,128)S(1)} custom-call(f32[1,128,128]{2,1,0:T(8,128)S(1)} %get-tuple-element.93), custom_call_target="InvertDiagBlocksLowerTriangular" | custom-call | tf_op jit(solution)/shard_map/jit(cholesky)/cholesky | solution.py:52
  288.1 12.1 %cholesky.465 = f32[128,128]{1,0:T(8,128)S(1)} custom-call(f32[128,128]{1,0:T(8,128)S(1)} %cholesky.603), custom_call_target="Cholesky" | custom-call | tf_op jit(solution)/shard_map/jit(cholesky)/cholesky | solution.py:52
  301.5 9.8 %custom-call.40 = f32[1,128,128]{1,2,0:T(8,128)S(1)} custom-call(f32[1,128,128]{2,1,0:T(8,128)S(1)} %get-tuple-element.90), custom_call_target="InvertDiagBlocksLowerTriangular" | custom-call | tf_op jit(solution)/shard_map/jit(cholesky)/cholesky | solution.py:52
  312.9 11.7 %cholesky.486 = f32[128,128]{1,0:T(8,128)S(1)} custom-call(f32[128,128]{1,0:T(8,128)S(1)} %cholesky.608), custom_call_target="Cholesky" | custom-call | tf_op jit(solution)/shard_map/jit(cholesky)/cholesky | solution.py:52
  325.4 9.8 %custom-call.41 = f32[1,128,128]{1,2,0:T(8,128)S(1)} custom-call(f32[1,128,128]{2,1,0:T(8,128)S(1)} %get-tuple-element.87), custom_call_target="InvertDiagBlocksLowerTriangular" | custom-call | tf_op jit(solution)/shard_map/jit(cholesky)/cholesky | solution.py:52
  336.6 11.9 %cholesky.503 = f32[128,128]{1,0:T(8,128)S(1)} custom-call(f32[128,128]{1,0:T(8,128)S(1)} %convolution_subtract_fusion.14), custom_call_target="Cholesky" | custom-call | tf_op jit(solution)/shard_map/jit(cholesky)/cholesky | solution.py:52
  352.9 11.4 %while.7 = (s32[]{:T(128)}, f32[512,512]{1,0:T(8,128)}, s32[4,2]{0,1:T(2,128)S(1)}, f32[4,128,128]{2,1,0:T(8,128)S(1)}, s32[]{:T(128)}) while((s32[]{:T(128)}, f32[512,512]{1,0:T(8,128)}, s32[4,2]{0,1:T(2,128)S(1)}, f32[4,128,128]{2,1,0:T(8,128)S(1)}, s32[]{:T(128)}) %tuple.105), condition=%wide.while_cond.clone, body=%wide.while_body.clone.sunk | while | flops 2 | bytes 131181 | solution.py:53
  364.3 39.3 %custom-call.42 = f32[4,128,128]{1,2,0:T(8,128)S(1)} custom-call(f32[4,128,128]{2,1,0:T(8,128)S(1)} %get-tuple-element.27), custom_call_target="InvertDiagBlocksLowerTriangular" | custom-call | tf_op jit(solution)/shard_map/jit(_solve_triangular)/triangular_solve | solution.py:53
  425.7 94.6 %all-gather.11.cloned.1.call-done = bf16[32,128,1024]{2,1,0:T(8,128)(2,1)} async-done(((bf16[1,128,1024]{2,1,0:T(8,128)(2,1)}), bf16[32,128,1024]{2,1,0:T(8,128)(2,1)}) %all-gather.11.cloned.1.call-update) | async-done | bytes 8388624 | tf_op jit(solution)/shard_map/all_gather | solution.py:74
  529.1 8.9 %fusion.4 = f32[32,1,128,4,128]{4,3,2,0,1:T(4,128)} fusion(s32[32,8]{1,0:T(8,128)S(1)} %copy.54, bf16[32,128,8,128]{3,2,1,0:T(8,128)(2,1)} %bitcast.244), kind=kOutput, calls=%fused_computation.10 | convolution fusion | flops 33555456 | bytes 16778240 | tf_op jit(solution)/shard_map/muvkc,mkb->muvbc/dot_general | solution.py:19
  538.0 10.3 %reshape.264 = f32[32,128,512]{2,1,0:T(8,128)} reshape(f32[32,1,128,4,128]{4,3,2,0,1:T(4,128)} %fusion.4) | data formatting | bytes 16777216 | tf_op jit(solution)/shard_map/reshape.65
  548.2 10.4 %fusion.2 = f32[4,128,512]{2,0,1:T(4,128)S(1)} fusion(f32[32,128,512]{2,1,0:T(8,128)} %reshape.264, s32[32]{0:T(128)S(1)} %get-tuple-element.112, pred[32]{0:T(512)(128)(4,1)S(1)} %broadcast_compare_fusion), kind=kOutput, calls=%fused_computation.8 | convolution fusion | flops 100663552 | bytes 9437344 | tf_op jit(solution)/shard_map/muvx,mut->tvx/dot_general | solution.py:34
  565.5 24.5 %all-gather.13.cloned.1.call-done = f32[1,1024,512]{1,2,0:T(8,128)} async-done(((f32[1,128,512]{1,2,0:T(8,128)}), f32[1,1024,512]{1,2,0:T(8,128)}) %all-gather.13.cloned.1.call-update) | async-done | bytes 2097168 | tf_op jit(solution)/shard_map/all_gather | solution.py:79
  593.1 11.7 %cholesky.518 = f32[128,128]{1,0:T(8,128)S(1)} custom-call(f32[128,128]{1,0:T(8,128)S(1)} %cholesky.612), custom_call_target="Cholesky" | custom-call | tf_op jit(solution)/shard_map/jit(cholesky)/cholesky | solution.py:80
  605.0 9.8 %custom-call.43 = f32[1,128,128]{1,2,0:T(8,128)S(1)} custom-call(f32[1,128,128]{2,1,0:T(8,128)S(1)} %get-tuple-element.83), custom_call_target="InvertDiagBlocksLowerTriangular" | custom-call | tf_op jit(solution)/shard_map/jit(cholesky)/cholesky | solution.py:80
  615.5 11.7 %cholesky.537 = f32[128,128]{1,0:T(8,128)S(1)} custom-call(f32[128,128]{1,0:T(8,128)S(1)} %cholesky.616), custom_call_target="Cholesky" | custom-call | tf_op jit(solution)/shard_map/jit(cholesky)/cholesky | solution.py:80
  628.6 10.0 %custom-call.44 = f32[1,128,128]{1,2,0:T(8,128)S(1)} custom-call(f32[1,128,128]{2,1,0:T(8,128)S(1)} %get-tuple-element.80), custom_call_target="InvertDiagBlocksLowerTriangular" | custom-call | tf_op jit(solution)/shard_map/jit(cholesky)/cholesky | solution.py:80
  639.2 11.7 %cholesky.558 = f32[128,128]{1,0:T(8,128)S(1)} custom-call(f32[128,128]{1,0:T(8,128)S(1)} %cholesky.621), custom_call_target="Cholesky" | custom-call | tf_op jit(solution)/shard_map/jit(cholesky)/cholesky | solution.py:80
  651.6 9.8 %custom-call.45 = f32[1,128,128]{1,2,0:T(8,128)S(1)} custom-call(f32[1,128,128]{2,1,0:T(8,128)S(1)} %get-tuple-element.77), custom_call_target="InvertDiagBlocksLowerTriangular" | custom-call | tf_op jit(solution)/shard_map/jit(cholesky)/cholesky | solution.py:80
  662.0 11.9 %cholesky.575 = f32[128,128]{1,0:T(8,128)S(1)} custom-call(f32[128,128]{1,0:T(8,128)S(1)} %convolution_subtract_fusion.13), custom_call_target="Cholesky" | custom-call | tf_op jit(solution)/shard_map/jit(cholesky)/cholesky | solution.py:80
  685.9 39.3 %custom-call.27 = f32[4,128,128]{1,2,0:T(8,128)S(1)} custom-call(f32[4,128,128]{2,1,0:T(8,128)S(1)} %get-tuple-element.19), custom_call_target="InvertDiagBlocksLowerTriangular" | custom-call | tf_op jit(solution)/shard_map/jit(_solve_triangular)/triangular_solve | solution.py:82
  (200 shorter events, 159.4 us)
Async XLA Ops:
  7.2 42.2 %all-gather.7.cloned.1.call-start = ((), (), s32[]{:S(2)}) async-start(), calls=%async_computation | async-start | bytes 4718592 | tf_op jit(solution)/shard_map/all_gather | solution.py:48
  9.1 238.2 %all-gather.9.cloned.1.call-start = ((), (), s32[]{:S(2)}) async-start(), calls=%async_computation.1 | async-start | bytes 4718592 | tf_op jit(solution)/shard_map/all_gather | solution.py:48
  58.9 1.9 copy-start
  193.8 5.7 copy-start.1
  206.0 1.6 copy-start.8
  207.4 5.1 copy-start.4
  212.5 307.8 %all-gather.11.cloned.1.call-start = ((), (), s32[]{:S(2)}) async-start(), calls=%async_computation.2 | async-start | bytes 8650752 | tf_op jit(solution)/shard_map/all_gather | solution.py:74
  256.9 1.9 copy-start.2
  262.9 1.0 copy-start.7
  403.6 5.8 copy-start.3
  418.8 2.4 copy-start.6
  418.9 3.7 copy-start.9
  419.2 5.0 copy-start.10
  419.2 5.0 copy-start.11
  419.3 6.3 copy-start.12
  422.5 167.6 %all-gather.13.cloned.1.call-start = ((), (), s32[]{:S(2)}) async-start(), calls=%async_computation.3 | async-start | bytes 2359296 | tf_op jit(solution)/shard_map/all_gather | solution.py:79
  558.7 3.5 copy-start.5
Sparse Core Ops, SparseCore 0:
  10.4 38.8 all-gather.6
  212.6 34.6 all-gather.8
  422.6 97.6 all-gather.10
  562.3 27.6 all-gather.12
where the time goes:
time: 747 us; the launch traced here: 737 us
  other arithmetic  369 us (49%)
  waiting for transfers between devices  193 us (26%)
  local copies, waits for them, and re-layouts  90.3 us (12%)
  matrix products  61.6 us (8%)
  between operations  22.8 us (3%)
    another operation x29, other arithmetic, on_device(): pivot_block = jnp.linalg.cholesky(gathered[first_col:trailing])  159 us
    all_gather x1, waiting for transfers between devices, on_device(): lax.all_gather(contribution[None], 'leaf', axis=0, tiled=True)  94.6 us
    another operation x5, other arithmetic, on_device(): jax.scipy.linalg.solve_triangular(pivot_block, gathered.T, lower=True)  79.9 us
    another operation x15, other arithmetic, on_device(): pivot_block = jnp.linalg.cholesky(stacked[:PANEL])  79.4 us
    all_gather x2, waiting for transfers between devices, on_device(): lax.all_gather(column.reshape(row_slots, 1, BLK, PANEL), 'panel', axis=1,...  73.8 us
    another operation x2, other arithmetic, on_device(): jax.scipy.linalg.solve_triangular(pivot_block, parent_rows.T, lower=True)  39.4 us
    unnamed x34, local copies, waits for them, and re-layouts  27 us
    all_gather x1, waiting for transfers between devices, on_device(): stacked = lax.all_gather(assembled[0], 'panel', axis=0, tiled=True)  24.5 us
  transfers between devices with their start and end apart: 4, of which 4 were waited for; matrix products, arithmetic and copies ran while one was open for 1% of the time, Pallas kernels for 0%

commit v1 on v0

--- a/solution.py
+++ b/solution.py
@@ -45,9 +45,24 @@
     for first_col in range(0, PC, PANEL):
         trailing = first_col + PANEL
         column = local_rows[:, first_col:trailing]
-        gathered = lax.all_gather(
-            column.reshape(row_slots, 1, BLK, PANEL), "panel", axis=1, tiled=True
-        )
+        x = column.reshape(row_slots, 1, BLK, PANEL)
+        ways, here, step = (lax.axis_size("panel"), lax.axis_index("panel"), x.shape[1])
+        shape = [n * ways if d == 1 else n for d, n in enumerate(x.shape)]
+        full = lax.dynamic_update_slice_in_dim(jnp.zeros(shape, x.dtype), x, here * step, axis=1)
+        going_up = going_down = x
+        for far in range(1, ways // 2 + 1):
+            going_up = lax.ppermute(going_up, "panel", [(d, (d + 1) % ways) for d in range(ways)])
+            full = lax.dynamic_update_slice_in_dim(
+                full, going_up, (here - far) % ways * step, axis=1
+            )
+            if 2 * far < ways:
+                going_down = lax.ppermute(
+                    going_down, "panel", [(d, (d - 1) % ways) for d in range(ways)]
+                )
+                full = lax.dynamic_update_slice_in_dim(
+                    full, going_down, (here + far) % ways * step, axis=1
+                )
+        gathered = full
         gathered = gathered.reshape(WC, PANEL)
         pivot_block = jnp.linalg.cholesky(gathered[first_col:trailing])
         all_rows = jax.scipy.linalg.solve_triangular(pivot_block, gathered.T, lower=True).T

time: 747 us -> 961 us (1.29)
  local copies, waits for them, and re-layouts: 90.3 us -> 316 us
  waiting for transfers between devices: 193 us -> 146 us
  starting transfers between devices: 0.16 us -> 36.1 us
    dynamic_update_slice x0 -> x16, local copies, waits for them, and re-layouts: none -> 233 us  [the longest x8 117 us: on_device(): lax.dynamic_update_slice_in_dim(full, going_up, (here - far) % ways * ste...]
    all_gather x2 -> x0, waiting for transfers between devices: 73.8 us -> none  [on_device(): lax.all_gather(column.reshape(row_slots, 1, BLK, PANEL), 'panel', axis=1,...]
    ppermute x0 -> x14, starting transfers between devices: none -> 36 us  [the longest x6 21.2 us: on_device(): lax.ppermute(going_down, 'panel', [(d, (d - 1) % ways) for d in range(way...]
    ppermute x0 -> x14, waiting for transfers between devices: none -> 18.4 us  [the longest x8 16.8 us: on_device(): lax.ppermute(going_up, 'panel', [(d, (d + 1) % ways) for d in range(ways)])]
    all_gather x2 -> x0, local copies, waits for them, and re-layouts: 10.9 us -> none  [on_device(): lax.all_gather(column.reshape(row_slots, 1, BLK, PANEL), 'panel', axis=1,...]
    another operation x13 -> x15, local copies, waits for them, and re-layouts: 18.7 us -> 23.1 us
    unnamed x34 -> x36, local copies, waits for them, and re-layouts: 27 us -> 27 us
  transfers between devices with their start and end apart: 4 -> 16, of which waited for: 4 -> 12; matrix products, arithmetic and copies ran while one was open for 1% -> 23% of each run, Pallas kernels for 0% -> 0%
where the time goes in v1:
time: 961 us; the launch traced here: 950 us
  other arithmetic  369 us (38%)
  local copies, waits for them, and re-layouts  316 us (33%)
  waiting for transfers between devices  146 us (15%)
  matrix products  60 us (6%)
  starting transfers between devices  36.1 us (4%)
  between operations  22.9 us (2%)
    another operation x29, other arithmetic, on_device(): pivot_block = jnp.linalg.cholesky(gathered[first_col:trailing])  159 us
    dynamic_update_slice x8, local copies, waits for them, and re-layouts, on_device(): lax.dynamic_update_slice_in_dim(full, going_up, (here - far) % ways * ste...  117 us
    all_gather x1, waiting for transfers between devices, on_device(): lax.all_gather(contribution[None], 'leaf', axis=0, tiled=True)  103 us
    dynamic_update_slice x6, local copies, waits for them, and re-layouts, on_device(): lax.dynamic_update_slice_in_dim(full, going_down, (here + far) % ways * s...  87.2 us
    another operation x5, other arithmetic, on_device(): jax.scipy.linalg.solve_triangular(pivot_block, gathered.T, lower=True)  79.9 us
    another operation x15, other arithmetic, on_device(): pivot_block = jnp.linalg.cholesky(stacked[:PANEL])  79.4 us
    another operation x2, other arithmetic, on_device(): jax.scipy.linalg.solve_triangular(pivot_block, parent_rows.T, lower=True)  39.4 us
    dynamic_update_slice x2, local copies, waits for them, and re-layouts, on_device(): lax.dynamic_update_slice_in_dim(jnp.zeros(shape, x.dtype), x, here * step...  29.1 us
  transfers between devices with their start and end apart: 16, of which 12 were waited for; matrix products, arithmetic and copies ran while one was open for 23% of the time, Pallas kernels for 0%

profile of v1, /device:TPU:1, one launch (start us, length us, event | category | flops | bytes accessed | tf_op | source)
XLA Modules:
  0.0 950.3 jit_solution(12834793237489840405)
XLA Ops:
  39.3 14.5 %dynamic_update_slice.48 = f32[2,8,128,512]{2,1,0,3:T(8,128)} dynamic-update-slice(f32[2,8,128,512]{2,1,0,3:T(8,128)} %broadcast.285.clone, f32[2,1,128,512]{2,1,0,3:T(1,128)S(1)} %copy.59, s32[]{:T(128)} %copy.165, s32[]{:T(128)S(6)} %select_n.108, s32[]{:T(128)} %copy.165, s32[]{:T(128)} %copy.165) | dynamic-update-slice | bytes 1048580 | tf_op jit(solution)/shard_map/dynamic_update_slice | solution.py:51
  53.8 14.5 %dynamic_update_slice.49 = f32[2,8,128,512]{2,1,0,3:T(8,128)} dynamic-update-slice(f32[2,8,128,512]{2,1,0,3:T(8,128)} %dynamic_update_slice.48, f32[2,1,128,512]{2,1,0,3:T(1,128)S(1)} %collective-permute-done, s32[]{:T(128)} %copy.165, s32[]{:T(128)S(6)} %select_n.110, s32[]{:T(128)} %copy.165, s32[]{:T(128)} %copy.165) | dynamic-update-slice | bytes 1048580 | tf_op jit(solution)/shard_map/dynamic_update_slice | solution.py:55
  68.4 14.5 %dynamic_update_slice.50 = f32[2,8,128,512]{2,1,0,3:T(8,128)} dynamic-update-slice(f32[2,8,128,512]{2,1,0,3:T(8,128)} %dynamic_update_slice.49, f32[2,1,128,512]{2,1,0,3:T(1,128)S(1)} %collective-permute-done.1, s32[]{:T(128)} %copy.165, s32[]{:T(128)S(6)} %select_n.112, s32[]{:T(128)} %copy.165, s32[]{:T(128)} %copy.165) | dynamic-update-slice | bytes 1048580 | tf_op jit(solution)/shard_map/dynamic_update_slice | solution.py:62
  82.9 14.5 %dynamic_update_slice.51 = f32[2,8,128,512]{2,1,0,3:T(8,128)} dynamic-update-slice(f32[2,8,128,512]{2,1,0,3:T(8,128)} %dynamic_update_slice.50, f32[2,1,128,512]{2,1,0,3:T(1,128)S(1)} %collective-permute-done.2, s32[]{:T(128)} %copy.165, s32[]{:T(128)S(6)} %select_n.114, s32[]{:T(128)} %copy.165, s32[]{:T(128)} %copy.165) | dynamic-update-slice | bytes 1048580 | tf_op jit(solution)/shard_map/dynamic_update_slice | solution.py:55
  97.4 14.5 %dynamic_update_slice.52 = f32[2,8,128,512]{2,1,0,3:T(8,128)} dynamic-update-slice(f32[2,8,128,512]{2,1,0,3:T(8,128)} %dynamic_update_slice.51, f32[2,1,128,512]{2,1,0,3:T(1,128)S(1)} %collective-permute-done.3, s32[]{:T(128)} %copy.165, s32[]{:T(128)S(6)} %select_n.116, s32[]{:T(128)} %copy.165, s32[]{:T(128)} %copy.165) | dynamic-update-slice | bytes 1048580 | tf_op jit(solution)/shard_map/dynamic_update_slice | solution.py:62
  111.9 14.5 %dynamic_update_slice.53 = f32[2,8,128,512]{2,1,0,3:T(8,128)} dynamic-update-slice(f32[2,8,128,512]{2,1,0,3:T(8,128)} %dynamic_update_slice.52, f32[2,1,128,512]{2,1,0,3:T(1,128)S(1)} %collective-permute-done.4, s32[]{:T(128)} %copy.165, s32[]{:T(128)S(6)} %select_n.118, s32[]{:T(128)} %copy.165, s32[]{:T(128)} %copy.165) | dynamic-update-slice | bytes 1048580 | tf_op jit(solution)/shard_map/dynamic_update_slice | solution.py:55
  126.5 14.5 %dynamic_update_slice.54 = f32[2,8,128,512]{2,1,0,3:T(8,128)} dynamic-update-slice(f32[2,8,128,512]{2,1,0,3:T(8,128)} %dynamic_update_slice.53, f32[2,1,128,512]{2,1,0,3:T(1,128)} %collective-permute-done.5, s32[]{:T(128)} %copy.165, s32[]{:T(128)S(6)} %select_n.120, s32[]{:T(128)} %copy.165, s32[]{:T(128)} %copy.165) | dynamic-update-slice | bytes 1048580 | tf_op jit(solution)/shard_map/dynamic_update_slice | solution.py:62
  141.0 15.0 %dynamic_update_slice.55 = f32[2,8,128,512]{2,1,0,3:T(8,128)} dynamic-update-slice(f32[2,8,128,512]{2,1,0,3:T(8,128)} %dynamic_update_slice.54, f32[2,1,128,512]{2,1,0,3:T(1,128)} %collective-permute-done.6, s32[]{:T(128)} %copy.165, s32[]{:T(128)S(6)} %select_n.122, s32[]{:T(128)} %copy.165, s32[]{:T(128)} %copy.165) | dynamic-update-slice | bytes 1048580 | tf_op jit(solution)/shard_map/dynamic_update_slice | solution.py:55
  164.0 11.7 %cholesky.374 = f32[128,128]{1,0:T(8,128)S(1)} custom-call(f32[128,128]{1,0:T(8,128)S(1)} %cholesky.586), custom_call_target="Cholesky" | custom-call | tf_op jit(solution)/shard_map/jit(cholesky)/cholesky | solution.py:67
  186.4 11.9 %cholesky.393 = f32[128,128]{1,0:T(8,128)S(1)} custom-call(f32[128,128]{1,0:T(8,128)S(1)} %cholesky.590), custom_call_target="Cholesky" | custom-call | tf_op jit(solution)/shard_map/jit(cholesky)/cholesky | solution.py:67
  208.8 11.7 %cholesky.414 = f32[128,128]{1,0:T(8,128)S(1)} custom-call(f32[128,128]{1,0:T(8,128)S(1)} %cholesky.595), custom_call_target="Cholesky" | custom-call | tf_op jit(solution)/shard_map/jit(cholesky)/cholesky | solution.py:67
  231.6 12.1 %cholesky.431 = f32[128,128]{1,0:T(8,128)S(1)} custom-call(f32[128,128]{1,0:T(8,128)S(1)} %convolution_subtract_fusion.11), custom_call_target="Cholesky" | custom-call | tf_op jit(solution)/shard_map/jit(cholesky)/cholesky | solution.py:67
  255.8 39.3 %custom-call.38 = f32[4,128,128]{1,2,0:T(8,128)S(1)} custom-call(f32[4,128,128]{2,1,0:T(8,128)S(1)} %get-tuple-element.26), custom_call_target="InvertDiagBlocksLowerTriangular" | custom-call | tf_op jit(solution)/shard_map/jit(_solve_triangular)/triangular_solve | solution.py:68
  341.4 14.5 %dynamic_update_slice.56 = f32[2,8,128,512]{2,1,0,3:T(8,128)} dynamic-update-slice(f32[2,8,128,512]{2,1,0,3:T(8,128)} %broadcast.285, f32[2,1,128,512]{2,1,0,3:T(1,128)S(1)} %copy.64, s32[]{:T(128)} %copy.165, s32[]{:T(128)S(6)} %select_n.108, s32[]{:T(128)} %copy.165, s32[]{:T(128)} %copy.165) | dynamic-update-slice | bytes 1048580 | tf_op jit(solution)/shard_map/dynamic_update_slice | solution.py:51
  356.0 14.5 %dynamic_update_slice.57 = f32[2,8,128,512]{2,1,0,3:T(8,128)} dynamic-update-slice(f32[2,8,128,512]{2,1,0,3:T(8,128)} %dynamic_update_slice.56, f32[2,1,128,512]{2,1,0,3:T(1,128)S(1)} %collective-permute-done.7, s32[]{:T(128)} %copy.165, s32[]{:T(128)S(6)} %select_n.110, s32[]{:T(128)} %copy.165, s32[]{:T(128)} %copy.165) | dynamic-update-slice | bytes 1048580 | tf_op jit(solution)/shard_map/dynamic_update_slice | solution.py:55
  370.5 14.5 %dynamic_update_slice.58 = f32[2,8,128,512]{2,1,0,3:T(8,128)} dynamic-update-slice(f32[2,8,128,512]{2,1,0,3:T(8,128)} %dynamic_update_slice.57, f32[2,1,128,512]{2,1,0,3:T(1,128)S(1)} %collective-permute-done.8, s32[]{:T(128)} %copy.165, s32[]{:T(128)S(6)} %select_n.112, s32[]{:T(128)} %copy.165, s32[]{:T(128)} %copy.165) | dynamic-update-slice | bytes 1048580 | tf_op jit(solution)/shard_map/dynamic_update_slice | solution.py:62
  385.0 14.5 %dynamic_update_slice.59 = f32[2,8,128,512]{2,1,0,3:T(8,128)} dynamic-update-slice(f32[2,8,128,512]{2,1,0,3:T(8,128)} %dynamic_update_slice.58, f32[2,1,128,512]{2,1,0,3:T(1,128)} %copy-done.9, s32[]{:T(128)} %copy.165, s32[]{:T(128)S(6)} %select_n.114, s32[]{:T(128)} %copy.165, s32[]{:T(128)} %copy.165) | dynamic-update-slice | bytes 1048580 | tf_op jit(solution)/shard_map/dynamic_update_slice | solution.py:55
  399.6 14.5 %dynamic_update_slice.60 = f32[2,8,128,512]{2,1,0,3:T(8,128)} dynamic-update-slice(f32[2,8,128,512]{2,1,0,3:T(8,128)} %dynamic_update_slice.59, f32[2,1,128,512]{2,1,0,3:T(1,128)} %collective-permute-done.10, s32[]{:T(128)} %copy.165, s32[]{:T(128)S(6)} %select_n.116, s32[]{:T(128)} %copy.165, s32[]{:T(128)} %copy.165) | dynamic-update-slice | bytes 1048580 | tf_op jit(solution)/shard_map/dynamic_update_slice | solution.py:62
  414.1 14.5 %dynamic_update_slice.61 = f32[2,8,128,512]{2,1,0,3:T(8,128)} dynamic-update-slice(f32[2,8,128,512]{2,1,0,3:T(8,128)} %dynamic_update_slice.60, f32[2,1,128,512]{2,1,0,3:T(1,128)} %collective-permute-done.11, s32[]{:T(128)} %copy.165, s32[]{:T(128)S(6)} %select_n.118, s32[]{:T(128)} %copy.165, s32[]{:T(128)} %copy.165) | dynamic-update-slice | bytes 1048580 | tf_op jit(solution)/shard_map/dynamic_update_slice | solution.py:55
  428.6 14.5 %dynamic_update_slice.62 = f32[2,8,128,512]{2,1,0,3:T(8,128)} dynamic-update-slice(f32[2,8,128,512]{2,1,0,3:T(8,128)} %dynamic_update_slice.61, f32[2,1,128,512]{2,1,0,3:T(1,128)} %collective-permute-done.12, s32[]{:T(128)} %copy.165, s32[]{:T(128)S(6)} %select_n.120, s32[]{:T(128)} %copy.165, s32[]{:T(128)} %copy.165) | dynamic-update-slice | bytes 1048580 | tf_op jit(solution)/shard_map/dynamic_update_slice | solution.py:62
  443.2 14.5 %dynamic_update_slice.63 = f32[2,8,128,512]{2,1,0,3:T(8,128)} dynamic-update-slice(f32[2,8,128,512]{2,1,0,3:T(8,128)} %dynamic_update_slice.62, f32[2,1,128,512]{2,1,0,3:T(1,128)} %collective-permute-done.13, s32[]{:T(128)} %copy.165, s32[]{:T(128)S(6)} %select_n.122, s32[]{:T(128)} %copy.165, s32[]{:T(128)} %copy.165) | dynamic-update-slice | bytes 1048580 | tf_op jit(solution)/shard_map/dynamic_update_slice | solution.py:55
  468.8 11.7 %cholesky.446 = f32[128,128]{1,0:T(8,128)S(1)} custom-call(f32[128,128]{1,0:T(8,128)S(1)} %cholesky.599), custom_call_target="Cholesky" | custom-call | tf_op jit(solution)/shard_map/jit(cholesky)/cholesky | solution.py:67
  493.1 12.1 %cholesky.465 = f32[128,128]{1,0:T(8,128)S(1)} custom-call(f32[128,128]{1,0:T(8,128)S(1)} %cholesky.603), custom_call_target="Cholesky" | custom-call | tf_op jit(solution)/shard_map/jit(cholesky)/cholesky | solution.py:67
  517.9 11.7 %cholesky.486 = f32[128,128]{1,0:T(8,128)S(1)} custom-call(f32[128,128]{1,0:T(8,128)S(1)} %cholesky.608), custom_call_target="Cholesky" | custom-call | tf_op jit(solution)/shard_map/jit(cholesky)/cholesky | solution.py:67
  541.6 11.9 %cholesky.503 = f32[128,128]{1,0:T(8,128)S(1)} custom-call(f32[128,128]{1,0:T(8,128)S(1)} %convolution_subtract_fusion.10), custom_call_target="Cholesky" | custom-call | tf_op jit(solution)/shard_map/jit(cholesky)/cholesky | solution.py:67
  569.3 39.3 %custom-call.42 = f32[4,128,128]{1,2,0:T(8,128)S(1)} custom-call(f32[4,128,128]{2,1,0:T(8,128)S(1)} %get-tuple-element.27), custom_call_target="InvertDiagBlocksLowerTriangular" | custom-call | tf_op jit(solution)/shard_map/jit(_solve_triangular)/triangular_solve | solution.py:68
  630.3 103.4 %all-gather.5.cloned.1.call-done = bf16[32,128,1024]{2,1,0:T(8,128)(2,1)} async-done(((bf16[1,128,1024]{2,1,0:T(8,128)(2,1)}), bf16[32,128,1024]{2,1,0:T(8,128)(2,1)}) %all-gather.5.cloned.1.call-update) | async-done | bytes 8388624 | tf_op jit(solution)/shard_map/all_gather | solution.py:89
  778.9 24.5 %all-gather.7.cloned.1.call-done = f32[1,1024,512]{1,2,0:T(8,128)} async-done(((f32[1,128,512]{1,2,0:T(8,128)}), f32[1,1024,512]{1,2,0:T(8,128)}) %all-gather.7.cloned.1.call-update) | async-done | bytes 2097168 | tf_op jit(solution)/shard_map/all_gather | solution.py:94
  806.6 11.7 %cholesky.518 = f32[128,128]{1,0:T(8,128)S(1)} custom-call(f32[128,128]{1,0:T(8,128)S(1)} %cholesky.612), custom_call_target="Cholesky" | custom-call | tf_op jit(solution)/shard_map/jit(cholesky)/cholesky | solution.py:95
  828.9 11.7 %cholesky.537 = f32[128,128]{1,0:T(8,128)S(1)} custom-call(f32[128,128]{1,0:T(8,128)S(1)} %cholesky.616), custom_call_target="Cholesky" | custom-call | tf_op jit(solution)/shard_map/jit(cholesky)/cholesky | solution.py:95
  875.5 11.9 %cholesky.575 = f32[128,128]{1,0:T(8,128)S(1)} custom-call(f32[128,128]{1,0:T(8,128)S(1)} %convolution_subtract_fusion.9), custom_call_target="Cholesky" | custom-call | tf_op jit(solution)/shard_map/jit(cholesky)/cholesky | solution.py:95
  899.3 39.3 %custom-call.27 = f32[4,128,128]{1,2,0:T(8,128)S(1)} custom-call(f32[4,128,128]{2,1,0:T(8,128)S(1)} %get-tuple-element.19), custom_call_target="InvertDiagBlocksLowerTriangular" | custom-call | tf_op jit(solution)/shard_map/jit(_solve_triangular)/triangular_solve | solution.py:97
  (242 shorter events, 345.8 us)
Async XLA Ops:
  7.2 726.6 %all-gather.5.cloned.1.call-start = ((), (), s32[]{:S(2)}) async-start(), calls=%async_computation | async-start | bytes 8650752 | tf_op jit(solution)/shard_map/all_gather | solution.py:89
  8.7 8.7 collective-permute-start
  11.3 8.9 collective-permute-start.1
  17.4 8.6 collective-permute-start.2
  20.2 8.9 collective-permute-start.3
  26.0 8.6 collective-permute-start.4
  29.1 97.4 %collective-permute-start.5 = (f32[2,1,128,512]{2,1,0,3:T(1,128)S(1)}, f32[2,1,128,512]{2,1,0,3:T(1,128)}, u32[]{:S(2)}, u32[]{:S(2)}) collective-permute-start(f32[2,1,128,512]{2,1,0,3:T(1,128)S(1)} %collective-permute-done.3), channel_id=1, source_target_pairs={{0,7},{1,0},{2,1},{3,2},{4,3},{5,4},{6,5},{7,6},{8,15},{9,8},{10,9... | collective-permute-start | bytes 1572872 | tf_op jit(solution)/shard_map/ppermute | solution.py:59
  34.6 106.4 %collective-permute-start.6 = (f32[2,1,128,512]{2,1,0,3:T(1,128)S(1)}, f32[2,1,128,512]{2,1,0,3:T(1,128)}, u32[]{:S(2)}, u32[]{:S(2)}) collective-permute-start(f32[2,1,128,512]{2,1,0,3:T(1,128)S(1)} %collective-permute-done.4), channel_id=1, source_target_pairs={{0,1},{1,2},{2,3},{3,4},{4,5},{5,6},{6,7},{7,0},{8,9},{9,10},{10,1... | collective-permute-start | bytes 1572872 | tf_op jit(solution)/shard_map/ppermute | solution.py:54
  160.2 1.9 copy-start
  295.1 3.4 copy-start.1
  306.1 1.6 copy-start.8
  307.5 4.3 copy-start.4
  312.2 6.1 collective-permute-start.7
  312.2 8.9 collective-permute-start.8
  318.3 9.4 collective-permute-start.9
  321.1 8.7 collective-permute-start.10
  327.7 2.1 copy-start.9
  327.7 9.9 %collective-permute-start.11 = (f32[2,1,128,512]{2,1,0,3:T(1,128)S(1)}, f32[2,1,128,512]{2,1,0,3:T(1,128)}, u32[]{:S(2)}, u32[]{:S(2)}) collective-permute-start(f32[2,1,128,512]{2,1,0,3:T(1,128)S(1)} %collective-permute-done.9), channel_id=1, source_target_pairs={{0,1},{1,2},{2,3},{3,4},{4,5},{5,6},{6,7},{7,0},{8,9},{9,10},{10,1... | collective-permute-start | bytes 1572872 | tf_op jit(solution)/shard_map/ppermute | solution.py:54
  329.8 98.8 %collective-permute-start.12 = (f32[2,1,128,512]{2,1,0,3:T(1,128)}, f32[2,1,128,512]{2,1,0,3:T(1,128)}, u32[]{:S(2)}, u32[]{:S(2)}) collective-permute-start(f32[2,1,128,512]{2,1,0,3:T(1,128)} %collective-permute-done.10), channel_id=1, source_target_pairs={{0,7},{1,0},{2,1},{3,2},{4,3},{5,4},{6,5},{7,6},{8,15},{9,8},{10,9... | collective-permute-start | bytes 1572872 | tf_op jit(solution)/shard_map/ppermute | solution.py:59
  337.7 105.5 %collective-permute-start.13 = (f32[2,1,128,512]{2,1,0,3:T(1,128)}, f32[2,1,128,512]{2,1,0,3:T(1,128)}, u32[]{:S(2)}, u32[]{:S(2)}) collective-permute-start(f32[2,1,128,512]{2,1,0,3:T(1,128)} %collective-permute-done.11), channel_id=1, source_target_pairs={{0,1},{1,2},{2,3},{3,4},{4,5},{5,6},{6,7},{7,0},{8,9},{9,10},{10,1... | collective-permute-start | bytes 1572872 | tf_op jit(solution)/shard_map/ppermute | solution.py:54
  461.9 1.9 copy-start.2
  467.9 1.0 copy-start.7
  608.6 4.3 copy-start.3
  623.4 2.4 copy-start.6
  623.4 3.7 copy-start.10
  623.8 5.0 copy-start.11
  623.8 5.0 copy-start.12
  623.8 6.3 copy-start.13
  627.0 176.4 %all-gather.7.cloned.1.call-start = ((), (), s32[]{:S(2)}) async-start(), calls=%async_computation.1 | async-start | bytes 2359296 | tf_op jit(solution)/shard_map/all_gather | solution.py:94
  772.1 3.5 copy-start.5
Sparse Core Ops, SparseCore 0:
  627.2 106.5 all-gather.4
  775.8 27.6 all-gather.6
